TPU v7x, 256 devices: a whole 4x4x8 slice. The times are simulated.
256 devices in a mesh: tm: 16 (over x, y), space: 16 (over z, core).
Axes of the slice: x: 4, y: 4, z: 8, core: 2. Of those that a mesh axis runs over, the one named last changes fastest.
Arguments:
- clip: bfloat16 [256, 512, 768], P('tm', 'space'), may hold values from -160 to 160
- w_spatial: bfloat16 [4, 768, 768], replicated, may hold values from -4 to 4
- w_temporal: bfloat16 [4, 768, 768], replicated, may hold values from -4 to 4
Outputs:
- result: bfloat16 [256, 512, 768], P('tm', 'space')
All inputs are finite; a program needn't handle non-finite values.
Results may differ from a plain program's by a relative error of at most 0.011.
Values may be sent and summed in bfloat16 or wider, within the bound.
A program may use at most 128 MiB of HBM per device.

v0:
```python
import math

import jax
import jax.numpy as jnp
from jax import lax
from jax.sharding import PartitionSpec as P

HEAD = 64


def rms_norm(values):
    wide = values.astype(jnp.float32)
    return (wide * lax.rsqrt(jnp.mean(wide * wide, axis=-1, keepdims=True) + 1e-06)).astype(
        jnp.bfloat16
    )


def project_three(normed, weights):
    width = normed.shape[-1]
    flat = normed.reshape(-1, width)
    stacked = jnp.einsum(
        "rd,jde->jre", flat, weights[:3], preferred_element_type=jnp.float32
    ).astype(jnp.bfloat16)
    return (
        stacked[0].reshape(normed.shape),
        stacked[1].reshape(normed.shape),
        stacked[2].reshape(normed.shape),
    )


def out_project(mixed, weight):
    width = mixed.shape[-1]
    return jnp.dot(mixed.reshape(-1, width), weight, preferred_element_type=jnp.float32).reshape(
        mixed.shape
    )


def attend_frame(parts):
    query, key, value = parts
    count, width = query.shape
    heads = width // HEAD
    qh = query.reshape(count, heads, HEAD)
    kh = key.reshape(count, heads, HEAD)
    vh = value.reshape(count, heads, HEAD)
    scores = jnp.einsum("qhd,khd->hqk", qh, kh, preferred_element_type=jnp.float32) * (
        1.0 / math.sqrt(HEAD)
    )
    largest = jnp.max(scores, axis=-1, keepdims=True)
    expo = jnp.exp(scores - largest)
    weights = (expo / jnp.sum(expo, axis=-1, keepdims=True)).astype(jnp.bfloat16)
    mixed = jnp.einsum("hqk,khd->qhd", weights, vh, preferred_element_type=jnp.float32)
    return mixed.astype(jnp.bfloat16).reshape(count, width)


def frame_block(parts):
    inner = (parts[0][0], parts[1][0], parts[2][0])
    return lax.map(attend_frame, inner)[None]


def on_device(clip, w_spatial, w_temporal):
    frames, toks, width = clip.shape
    heads = width // HEAD
    space_count = lax.axis_size("space")
    frame_shape = (space_count, frames // space_count, toks, width)
    normed = rms_norm(clip)
    sq, sk, sv = project_three(normed, w_spatial)
    smix = frame_block(
        (
            lax.all_to_all(
                sq.reshape(frame_shape), "space", split_axis=0, concat_axis=2, tiled=True
            ),
            lax.all_to_all(
                sk.reshape(frame_shape), "space", split_axis=0, concat_axis=2, tiled=True
            ),
            lax.all_to_all(
                sv.reshape(frame_shape), "space", split_axis=0, concat_axis=2, tiled=True
            ),
        )
    )
    smix = lax.all_to_all(smix, "space", split_axis=2, concat_axis=0, tiled=True).reshape(
        frames, toks, width
    )
    after_space = (clip.astype(jnp.float32) + out_project(smix, w_spatial[3])).astype(jnp.bfloat16)
    tnormed = rms_norm(after_space)
    tq, tk, tv = project_three(tnormed, w_temporal)
    first_frame = lax.axis_index("tm") * frames
    qh = tq.reshape(frames, toks, heads, HEAD)
    query_pos = first_frame + jnp.arange(frames, dtype=jnp.int32)
    running = jnp.full((frames, toks, heads), -1e30, jnp.float32)
    key_piece = lax.all_gather(tk, "tm", axis=0, tiled=True)
    value_piece = lax.all_gather(tv, "tm", axis=0, tiled=True)
    count = key_piece.shape[0]
    kh = key_piece.reshape(count, toks, heads, HEAD)
    vh = value_piece.reshape(count, toks, heads, HEAD)
    scores = jnp.einsum("fphd,gphd->fphg", qh, kh, preferred_element_type=jnp.float32) * (
        1.0 / math.sqrt(HEAD)
    )
    key_pos = jnp.arange(count, dtype=jnp.int32)
    allowed = (key_pos[None, :] <= query_pos[:, None])[:, None, None, :]
    scores = jnp.where(allowed, scores, -1e30)
    newmax = jnp.maximum(running, jnp.max(scores, axis=-1))
    expo = jnp.where(allowed, jnp.exp(scores - newmax[..., None]), 0.0)
    total = jnp.sum(expo, axis=-1)
    acc = jnp.einsum("fphg,gphd->fphd", expo, vh.astype(jnp.float32))
    running, total, acc = (newmax, total, acc)
    tmix = (acc / total[..., None]).reshape(frames, toks, width).astype(jnp.bfloat16)
    return (after_space.astype(jnp.float32) + out_project(tmix, w_temporal[3])).astype(jnp.bfloat16)


def solution(mesh):
    placed = (P("tm", "space", None), P(), P())
    return jax.shard_map(
        on_device, mesh=mesh, in_specs=placed, out_specs=P("tm", "space", None), check_vma=False
    )
```

profile of v0, /device:TPU:1, one launch (start us, length us, event | category | flops | bytes accessed | tf_op | source)
XLA Modules:
  0.0 389.2 jit_solution(14649983245477244457)
XLA Ops:
  6.5 1.4 fusion.23
  7.9 1.3 fusion.24
  9.2 4.0 %convert_bitcast_fusion.1 = bf16[3,512,768]{2,1,0:T(8,128)(2,1)S(1)} fusion(bf16[512,768,1]{1,0,2:T(8,128)(2,1)S(1)} %bitcast.74, bf16[4,768,768]{2,1,0:T(8,128)(2,1)} %param.4), kind=kOutput, calls=%fused_computation.30 | convolution fusion | flops 1813118976 | bytes 6684672 | tf_op jit(solution)/shard_map/rd,jde->jre/dot_general | solution.py:21
  13.3 1.0 fusion.54
  14.3 32.7 %all_to_all.16 = bf16[16,1,32,768]{3,2,1,0:T(8,128)(2,1)} all-to-all(bf16[16,1,32,768]{3,2,1,0:T(8,128)(2,1)S(1)} %bitcast.73), channel_id=1, replica_groups=mesh['tm'=16,'space'=16] {'space'}, dimensions={0} | all-to-all | bytes 1572864 | tf_op jit(solution)/shard_map/all_to_all | solution.py:69
  47.0 25.7 %all_to_all.17 = bf16[16,1,32,768]{3,2,1,0:T(8,128)(2,1)} all-to-all(bf16[16,1,32,768]{3,2,1,0:T(8,128)(2,1)S(1)} %bitcast.72), channel_id=1, replica_groups=mesh['tm'=16,'space'=16] {'space'}, dimensions={0} | all-to-all | bytes 1572864 | tf_op jit(solution)/shard_map/all_to_all | solution.py:72
  72.7 3.5 all-to-all-start
  76.4 2.7 reshape.105
  79.1 3.8 reshape.106
  82.9 8.0 %fusion.32 = f32[12,512,512]{1,2,0:T(8,128)} fusion(bf16[512,12,64]{2,1,0:T(8,128)(2,1)} %reshape.106, bf16[512,12,64]{2,1,0:T(8,128)(2,1)S(1)} %reshape.105), kind=kOutput, calls=%fused_computation.40 | convolution fusion | flops 402653184 | bytes 14155776 | tf_op jit(solution)/shard_map/while/body/eval_jaxpr/qhd,khd->hqk/dot_general | solution.py:45
  90.9 11.1 %fusion.55 = f32[12,512]{1,0:T(8,128)S(1)} fusion(f32[12,512,512]{1,2,0:T(8,128)} %fusion.32), kind=kOutput, calls=%fused_computation.61 | output fusion | flops 12583423 | bytes 12607488 | tf_op jit(solution)/shard_map/while/body/eval_jaxpr/sub | solution.py:49
  102.1 1.3 reshape.104
  103.4 12.5 %fusion.35 = bf16[12,64,512]{2,1,0:T(8,128)(2,1)S(1)} fusion(f32[12,512]{1,0:T(8,128)S(1)} %fusion.55, bf16[512,12,64]{2,1,0:T(8,128)(2,1)S(1)} %reshape.104, f32[12,512,512]{1,2,0:T(8,128)} %fusion.32), kind=kOutput, calls=%fused_computation.43 | convolution fusion | flops 418781696 | bytes 14180352 | tf_op jit(solution)/shard_map/while/body/eval_jaxpr/hqk,khd->qhd/dot_general | solution.py:51
  115.8 1.8 copy.40
  118.2 5.5 %reduce = bf16[512,768]{1,0:T(8,128)(2,1)S(1)} reduce(bf16[512,1,1,768]{3,2,1,0:T(2,128)(2,1)S(1)} %bitcast.68, bf16[]{:T(256)} %broadcast.73), dimensions={1,2}, to_apply=%bitcast.56.reduce_sub_computation | reduce | bytes 1572866
  123.9 29.7 %all_to_all.18 = bf16[16,2,12288]{2,1,0:T(2,128)(2,1)S(1)} all-to-all(bf16[16,2,12288]{2,1,0:T(2,128)(2,1)S(1)} %reshape.114), channel_id=1, replica_groups=mesh['tm'=16,'space'=16] {'space'}, dimensions={0} | all-to-all | bytes 1572864 | tf_op jit(solution)/shard_map/all_to_all | solution.py:80
  153.5 0.7 reshape.115
  154.4 2.2 fusion.26
  157.5 4.0 %convert_bitcast_fusion = bf16[3,512,768]{2,1,0:T(8,128)(2,1)S(1)} fusion(bf16[512,768,1]{1,0,2:T(8,128)(2,1)S(1)} %bitcast.75, bf16[4,768,768]{2,1,0:T(8,128)(2,1)} %param.5), kind=kOutput, calls=%fused_computation.29 | convolution fusion | flops 1813118976 | bytes 6684672 | tf_op jit(solution)/shard_map/rd,jde->jre/dot_general | solution.py:21
  161.5 1.4 fusion.53
  162.9 0.7 all-gather.3.cloned.1.call-update
  163.7 1.5 reshape_reshape_squeeze.15
  165.2 89.3 %all-gather.5.cloned.1.call-done = bf16[256,32,768]{2,1,0:T(8,128)(2,1)} async-done(((bf16[16,32,768]{2,1,0:T(8,128)(2,1)}), bf16[256,32,768]{2,1,0:T(8,128)(2,1)}) %all-gather.5.cloned.1.call-update) | async-done | bytes 12582928 | tf_op jit(solution)/shard_map/all_gather | solution.py:90
  254.5 16.7 %copy.42 = bf16[256,32,768]{0,2,1:T(8,128)(2,1)} copy(bf16[256,32,768]{2,1,0:T(8,128)(2,1)} %all-gather.5.cloned.1.call-done) | data formatting | bytes 25165824 | tf_op jit(solution)/shard_map/all_gather | solution.py:90
  271.1 6.0 %fusion.6 = (f32[16,32,12]{0,2,1:T(8,128)S(1)}, f32[32,12,256,16]{2,3,1,0:T(8,128)S(1)}) fusion(pred[16,256]{1,0:T(8,128)(4,1)S(1)} %iota_compare_fusion, bf16[256,32,12,64]{0,3,2,1:T(8,128)(2,1)} %bitcast.66, bf16[16,32,12,64]{3,2,1,0:T(8,128)(2,1)S(1)} %reshape_reshape_squeeze.15), kind=kOutput, calls=%fused_computation.9 | convolution fusion | flops 206039040 | bytes 19689472 | tf_op jit(solution)/shard_map/fphd,gphd->fphg/dot_general | solution.py:95
  277.2 2.7 copy-done
  279.9 2.1 fusion.7
  282.0 69.5 %all-gather.3.cloned.1.call-done = bf16[256,32,768]{2,1,0:T(8,128)(2,1)} async-done(((bf16[16,32,768]{2,1,0:T(8,128)(2,1)}), bf16[256,32,768]{2,1,0:T(8,128)(2,1)}) %all-gather.3.cloned.1.call-update) | async-done | bytes 12582928 | tf_op jit(solution)/shard_map/all_gather | solution.py:91
  351.5 16.7 %copy.41 = bf16[256,32,768]{0,2,1:T(8,128)(2,1)} copy(bf16[256,32,768]{2,1,0:T(8,128)(2,1)} %all-gather.3.cloned.1.call-done) | data formatting | bytes 25165824 | tf_op jit(solution)/shard_map/all_gather | solution.py:91
  368.3 8.3 %fusion.13 = bf16[16,32,12,64]{3,0,2,1:T(8,128)(2,1)S(1)} fusion(f32[16,32,12]{0,2,1:T(8,128)S(1)} %fusion.7, bf16[256,32,12,64]{0,3,2,1:T(8,128)(2,1)} %bitcast.67, f32[32,12,256,16]{2,3,1,0:T(8,128)} %copy-done, f32[16,32,12]{0,2,1:T(8,128)S(1)} %broadcast_maximum_fusion, pred[16,256]{1,0:T(8,128)(4,1)S(1)} %iota_compare_fusion), kind=kOutput, calls=%fused_computation.17 | convolution fusion | flops 208404480 | bytes 19714048 | tf_op jit(solution)/shard_map/fphg,gphd->fphd/dot_general | solution.py:104
  377.1 2.0 convert_element_type.65
  379.2 3.2 fusion.28
  (21 shorter events, 2.6 us)
Async XLA Ops:
  72.7 29.4 %all-to-all-start = ((bf16[16,1,32,768]{3,2,1,0:T(8,128)(2,1)}), bf16[16,1,32,768]{3,2,1,0:T(8,128)(2,1)S(1)}, u32[]{:S(2)}, u32[]{:S(2)}) async-start(bf16[16,1,32,768]{3,2,1,0:T(8,128)(2,1)} %bitcast.4), calls=%async_computation | async-start | bytes 1572864 | tf_op jit(solution)/shard_map/all_to_all | solution.py:75
  76.2 178.3 %all-gather.5.cloned.1.call-start = ((), (), s32[]{:S(2)}) async-start(), calls=%async_computation.5 | async-start | bytes 13369344 | tf_op jit(solution)/shard_map/all_gather | solution.py:90
  118.2 36.2 %copy-start.1 = (bf16[16,32,768]{2,1,0:T(8,128)(2,1)S(1)}, bf16[16,32,768]{2,1,0:T(8,128)(2,1)}, u32[]{:S(2)}) copy-start(bf16[16,32,768]{2,1,0:T(8,128)(2,1)} %param.3) | copy-start | bytes 2359300
  156.6 0.9 copy-start.2
  162.9 188.6 %all-gather.3.cloned.1.call-start = ((), (), s32[]{:S(2)}) async-start(), calls=%async_computation.4 | async-start | bytes 13369344 | tf_op jit(solution)/shard_map/all_gather | solution.py:91
  277.2 2.7 copy-start
  376.6 2.6 copy-start.3
Sparse Core Ops, SparseCore 0:
  163.0 91.4 all-gather.4
  256.9 94.5 all-gather.2
where the time goes:
time: 391 us; the launch traced here: 389 us
  waiting for transfers between devices  159 us (41%)
  blocking collectives  88 us (23%)
  local copies, waits for them, and re-layouts  54.3 us (14%)
  matrix products  48.2 us (12%)
  other arithmetic  21.7 us (6%)
  between operations  13.6 us (3%)
    all_gather x1, waiting for transfers between devices, on_device(): key_piece = lax.all_gather(tk, 'tm', axis=0, tiled=True)  89.3 us
    all_gather x1, waiting for transfers between devices, on_device(): value_piece = lax.all_gather(tv, 'tm', axis=0, tiled=True)  69.5 us
    all_to_all x1, blocking collectives, on_device(): lax.all_to_all(sq.reshape(frame_shape), 'space', split_axis=0, concat_axi...  32.7 us
    all_to_all x1, blocking collectives, on_device(): lax.all_to_all(smix, 'space', split_axis=2, concat_axis=0, tiled=True)  29.7 us
    all_to_all x1, blocking collectives, on_device(): lax.all_to_all(sk.reshape(frame_shape), 'space', split_axis=0, concat_axi...  25.7 us
    all_gather x1, local copies, waits for them, and re-layouts, on_device(): value_piece = lax.all_gather(tv, 'tm', axis=0, tiled=True)  16.7 us
    all_gather x1, local copies, waits for them, and re-layouts, on_device(): key_piece = lax.all_gather(tk, 'tm', axis=0, tiled=True)  16.7 us
    dot_general x1, matrix products, attend_frame(): jnp.einsum('hqk,khd->qhd', weights, vh, preferred_element_type=jnp.float32)  12.5 us
  transfers between devices with their start and end apart: 3, of which 2 were waited for; matrix products, arithmetic and copies ran while one was open for 13% of the time, Pallas kernels for 0%

commit v1 on v0

v1 whole, which is shorter than its diff:
```python
import functools
import math

import jax
import jax.numpy as jnp
from jax import lax
from jax.experimental import pallas as pl
from jax.experimental.pallas import tpu as pltpu
from jax.sharding import PartitionSpec as P

MESH = pl.DeviceIdType.MESH
HEAD = 64
LANES = 128
WIDTH = 768
PAIRS = WIDTH // LANES
SCALE = math.log2(math.e) / math.sqrt(HEAD)
BF16 = jnp.bfloat16
F32 = jnp.float32

Z_OFFS = [(0, 0), (0, 1)]
for _far in (1, -1, 2, -2, 3, -3, 4):
    Z_OFFS += [(_far, 0), (_far, 1)]
Z_INV = [Z_OFFS.index((dz if dz == 4 else -dz, dc)) for dz, dc in Z_OFFS]
T_OFFS = [(dx, dy) for dx in (0, 1, 3, 2) for dy in (0, 1, 3, 2)]
T_INV = [T_OFFS.index(((-dx) % 4, (-dy) % 4)) for dx, dy in T_OFFS]

Z_GROUPS = ((0, 2), (2, 6), (6, 10), (10, 14), (14, 16))
A_SENDS = list(range(15, 0, -1))


def z_peer(me, slot):
    dz, dc = Z_OFFS[slot]
    return lax.rem(me // 2 + (dz + 8), 8) * 2 + lax.rem(lax.rem(me, 2) + dc, 2)


def t_peer(me, slot):
    dx, dy = T_OFFS[slot]
    return lax.rem(me // 4 + dx, 4) * 4 + lax.rem(lax.rem(me, 4) + dy, 4)


def normed_rows(rows):
    wide = rows.astype(F32)
    return (wide * lax.rsqrt(jnp.mean(wide * wide, axis=-1, keepdims=True) + 1e-06)).astype(BF16)


def dot(a, b):
    return jnp.dot(a, b, preferred_element_type=F32)


def attend(q, k, vx, mask):
    n = q.shape[0] // 2
    scores = lax.dot_general(q, k, (((1,), (1,)), ((), ())), preferred_element_type=F32)
    if mask is not None:
        scores = jnp.where(mask, scores, -1e30)
    largest = jnp.max(scores, axis=-1, keepdims=True)
    expo = jnp.exp2(scores - largest).astype(BF16)
    both = dot(expo, vx)
    both = both[:, :LANES] / both[:, LANES:]
    lane = lax.broadcasted_iota(jnp.int32, (n, LANES), 1)
    return jnp.where(lane < HEAD, both[:n], both[n:]).astype(BF16)


def kernel(
    clip, w_space, w_time, out,
    ws, wt, x, q2, k, vx, mix, after, home, perm, grouped, series,
    tq2, tk, tvx, tmix, answer, back, final,
    w_sem, a_send, a_recv, b_send, b_recv, c_send, c_recv, d_send, d_recv, own_sem, out_sem,
):
    t_me = lax.axis_index("tm")
    s_me = lax.axis_index("space")

    loads = [pltpu.make_async_copy(w_space, ws, w_sem.at[0]), pltpu.make_async_copy(w_time, wt, w_sem.at[1])]
    own_a = pltpu.make_async_copy(clip.at[s_me], x.at[0], own_sem.at[0])
    own_a.start()
    for load in loads:
        load.start()

    barrier = pltpu.get_barrier_semaphore()
    for slot in range(1, 16):
        pl.semaphore_signal(barrier, inc=1, device_id={"space": z_peer(s_me, slot)}, device_id_type=MESH)
        pl.semaphore_signal(barrier, inc=1, device_id={"tm": t_peer(t_me, slot)}, device_id_type=MESH)
    pl.semaphore_wait(barrier, 30)

    def a_copy(slot):
        peer = z_peer(s_me, slot)
        return pltpu.make_async_remote_copy(
            src_ref=clip.at[peer], dst_ref=x.at[Z_INV[slot]],
            send_sem=a_send.at[slot], recv_sem=a_recv.at[Z_INV[slot]],
            device_id={"space": peer}, device_id_type=MESH,
        )

    for slot in A_SENDS:
        a_copy(slot).start()

    ones = jnp.ones((512, LANES), BF16)
    for pair in range(PAIRS):
        vx[pair, :, LANES:] = ones
        tvx[pair, :, LANES:] = ones[:256]
    row = lax.broadcasted_iota(jnp.int32, (256, 256), 0)
    col = lax.broadcasted_iota(jnp.int32, (256, 256), 1)
    swap = (row // 16 == col % 16) & (row % 16 == col // 16)
    perm[...] = jnp.where(swap, 1.0, 0.0).astype(BF16)
    lane = lax.broadcasted_iota(jnp.int32, (1, WIDTH), 1)
    first = jnp.where(lane % LANES < HEAD, SCALE, 0.0).astype(F32)
    second = jnp.where(lane % LANES < HEAD, 0.0, SCALE).astype(F32)

    loads[0].wait()
    own_a.wait()
    for lo, hi in Z_GROUPS:
        for slot in range(max(lo, 1), hi):
            pltpu.make_async_remote_copy(
                src_ref=clip.at[0], dst_ref=x.at[slot], send_sem=a_send.at[slot], recv_sem=a_recv.at[slot],
                device_id={"space": z_peer(s_me, slot)}, device_id_type=MESH,
            ).wait_recv()
        count = hi - lo
        normed = normed_rows(x[lo:hi].reshape(count * 32, WIDTH))
        for index in range(3):
            made = dot(normed, ws[index])
            if index == 0:
                kinds = [((made * first).astype(BF16), q2, 0), ((made * second).astype(BF16), q2, 1)]
            else:
                kinds = [(made.astype(BF16), (k, vx)[index - 1], None)]
            for value, ref, head in kinds:
                value = value.reshape(count, 2, 16, WIDTH)
                for th in range(2):
                    part = value[:, th].reshape(count * 16, WIDTH)
                    at = pl.ds(th * 256 + lo * 16, count * 16)
                    for pair in range(PAIRS):
                        piece = part[:, pair * LANES:(pair + 1) * LANES]
                        if head is None:
                            ref[pair, at, :LANES] = piece
                        else:
                            ref[pair, head, at, :] = piece

    def b_copy(th, slot):
        peer = z_peer(s_me, slot)
        return pltpu.make_async_remote_copy(
            src_ref=after.at[th, slot], dst_ref=home.at[th, s_me],
            send_sem=b_send.at[th, slot], recv_sem=b_recv.at[th, Z_INV[slot]],
            device_id={"space": peer}, device_id_type=MESH,
        )

    def c_copy(th, slot):
        peer = t_peer(t_me, slot)
        return pltpu.make_async_remote_copy(
            src_ref=grouped.at[th, peer], dst_ref=series.at[th, t_me],
            send_sem=c_send.at[th, slot], recv_sem=c_recv.at[th, T_INV[slot]],
            device_id={"tm": peer}, device_id_type=MESH,
        )

    def d_copy(th, slot):
        peer = t_peer(t_me, slot)
        return pltpu.make_async_remote_copy(
            src_ref=answer.at[th, peer], dst_ref=back.at[th, t_me],
            send_sem=d_send.at[th, slot], recv_sem=d_recv.at[th, T_INV[slot]],
            device_id={"tm": peer}, device_id_type=MESH,
        )

    own_b = [pltpu.make_async_copy(after.at[th, 0], home.at[th, s_me], own_sem.at[1 + th]) for th in range(2)]
    own_c = [pltpu.make_async_copy(grouped.at[th, t_me], series.at[th, t_me], own_sem.at[3 + th]) for th in range(2)]
    own_d = [pltpu.make_async_copy(answer.at[th, t_me], back.at[th, t_me], own_sem.at[5 + th]) for th in range(2)]

    def space_block(th, half):
        base = th * 256 + half * 128

        def one(pair, carry):
            q = q2[pair, :, base:base + 128, :].reshape(256, LANES)
            mixed = attend(q, k[pair], vx[pair], None)
            mix[:, pl.ds(pl.multiple_of(pair * LANES, LANES), LANES)] = mixed
            return carry

        lax.fori_loop(0, PAIRS, one, 0)
        held = x[half * 8:half * 8 + 8, th * 16:th * 16 + 16, :].reshape(128, WIDTH).astype(F32)
        done = (held + dot(mix[...], ws[3])).astype(BF16)
        after[th, half * 8:half * 8 + 8] = done.reshape(8, 16, WIDTH)
        for slot in range(half * 8 + 7, half * 8 - 1, -1):
            if slot == 0:
                own_b[th].start()
            else:
                b_copy(th, slot).start()

    def regroup(th):
        own_b[th].wait()
        for slot in range(1, 16):
            pltpu.make_async_remote_copy(
                src_ref=after.at[th, slot], dst_ref=home.at[th, z_peer(s_me, slot)],
                send_sem=b_send.at[th, slot], recv_sem=b_recv.at[th, slot],
                device_id={"space": z_peer(s_me, slot)}, device_id_type=MESH,
            ).wait_recv()
        moved = dot(perm[...], home[th].reshape(256, WIDTH)).astype(BF16)
        grouped[th] = moved.reshape(16, 16, WIDTH)
        own_c[th].start()
        for slot in range(1, 16):
            c_copy(th, slot).start()

    def time_project(th):
        own_c[th].wait()
        for slot in range(1, 16):
            pltpu.make_async_remote_copy(
                src_ref=grouped.at[th, 0], dst_ref=series.at[th, t_peer(t_me, slot)],
                send_sem=c_send.at[th, slot], recv_sem=c_recv.at[th, slot],
                device_id={"tm": t_peer(t_me, slot)}, device_id_type=MESH,
            ).wait_recv()
        normed = normed_rows(series[th].reshape(256, WIDTH))
        for index in range(3):
            made = dot(normed, wt[index])
            for pair in range(PAIRS):
                cols = slice(pair * LANES, (pair + 1) * LANES)
                if index == 0:
                    tq2[pair, 0] = (made[:, cols] * first[:, cols]).astype(BF16)
                    tq2[pair, 1] = (made[:, cols] * second[:, cols]).astype(BF16)
                elif index == 1:
                    tk[pair] = made[:, cols].astype(BF16)
                else:
                    tvx[pair, :, :LANES] = made[:, cols].astype(BF16)

    def time_block(th, half):
        keys = 128 * (half + 1)
        query = lax.broadcasted_iota(jnp.int32, (256, keys), 0) % 128 + 128 * half
        mask = lax.broadcasted_iota(jnp.int32, (256, keys), 1) <= query

        def one(pair, carry):
            q = tq2[pair, :, half * 128:half * 128 + 128, :].reshape(256, LANES)
            mixed = attend(q, tk[pair, :keys, :], tvx[pair, :keys, :], mask)
            tmix[:, pl.ds(pl.multiple_of(pair * LANES, LANES), LANES)] = mixed
            return carry

        lax.fori_loop(0, PAIRS, one, 0)
        held = series[th, half * 8:half * 8 + 8].reshape(128, WIDTH).astype(F32)
        done = (held + dot(tmix[...], wt[3])).astype(BF16)
        answer[th, half * 8:half * 8 + 8] = done.reshape(8, 16, WIDTH)

    def send_answer(th):
        own_d[th].start()
        for slot in range(1, 16):
            d_copy(th, slot).start()

    outs = [
        pltpu.make_async_copy(final.at[th], out.at[:, pl.ds(th * 16, 16), :], out_sem.at[th]) for th in range(2)
    ]

    def finish(th):
        own_d[th].wait()
        for slot in range(1, 16):
            pltpu.make_async_remote_copy(
                src_ref=answer.at[th, 0], dst_ref=back.at[th, t_peer(t_me, slot)],
                send_sem=d_send.at[th, slot], recv_sem=d_recv.at[th, slot],
                device_id={"tm": t_peer(t_me, slot)}, device_id_type=MESH,
            ).wait_recv()
        moved = dot(perm[...], back[th].reshape(256, WIDTH)).astype(BF16)
        final[th] = moved.reshape(16, 16, WIDTH)
        outs[th].start()

    for th in range(2):
        space_block(th, 1)
        space_block(th, 0)
    regroup(0)
    loads[1].wait()
    time_project(0)
    time_block(0, 0)
    time_block(0, 1)
    regroup(1)
    send_answer(0)
    time_project(1)
    time_block(1, 0)
    time_block(1, 1)
    send_answer(1)
    finish(0)
    finish(1)

    for slot in range(1, 16):
        a_copy(slot).wait_send()
        for th in range(2):
            b_copy(th, slot).wait_send()
            c_copy(th, slot).wait_send()
            d_copy(th, slot).wait_send()
    for copy in outs:
        copy.wait()


def on_device(clip, w_spatial, w_temporal):
    dma = pltpu.SemaphoreType.DMA
    vmem = pltpu.VMEM
    return pl.pallas_call(
        kernel,
        out_shape=jax.ShapeDtypeStruct(clip.shape, BF16),
        in_specs=[pl.BlockSpec(memory_space=pl.ANY)] * 3,
        out_specs=pl.BlockSpec(memory_space=pl.ANY),
        scratch_shapes=[
            vmem((4, WIDTH, WIDTH), BF16),
            vmem((4, WIDTH, WIDTH), BF16),
            vmem((16, 32, WIDTH), BF16),
            vmem((PAIRS, 2, 512, LANES), BF16),
            vmem((PAIRS, 512, LANES), BF16),
            vmem((PAIRS, 512, 2 * LANES), BF16),
            vmem((128, WIDTH), BF16),
            vmem((2, 16, 16, WIDTH), BF16),
            vmem((2, 16, 16, WIDTH), BF16),
            vmem((256, 256), BF16),
            vmem((2, 16, 16, WIDTH), BF16),
            vmem((2, 16, 16, WIDTH), BF16),
            vmem((PAIRS, 2, 256, LANES), BF16),
            vmem((PAIRS, 256, LANES), BF16),
            vmem((PAIRS, 256, 2 * LANES), BF16),
            vmem((128, WIDTH), BF16),
            vmem((2, 16, 16, WIDTH), BF16),
            vmem((2, 16, 16, WIDTH), BF16),
            vmem((2, 16, 16, WIDTH), BF16),
            dma((2,)),
            dma((16,)), dma((16,)),
            dma((2, 16)), dma((2, 16)),
            dma((2, 16)), dma((2, 16)),
            dma((2, 16)), dma((2, 16)),
            dma((7,)),
            dma((2,)),
        ],
        compiler_params=pltpu.CompilerParams(
            collective_id=0, has_side_effects=True, vmem_limit_bytes=60 * 1024 * 1024
        ),
    )(clip, w_spatial, w_temporal)


def solution(mesh):
    placed = (P("tm", "space", None), P(), P())
    return jax.shard_map(
        on_device, mesh=mesh, in_specs=placed, out_specs=P("tm", "space", None), check_vma=False
    )
```

time: 391 us -> 89.9 us (0.23)
  the two profiles are of different devices: /device:TPU:1 before, /device:TPU:8 now
where the time goes in v1:
time: 89.9 us; the launch traced here: 89.8 us
  Pallas kernels  87.7 us (98%)
  local copies, waits for them, and re-layouts  2.06 us (2%)
    pallas_call x1, Pallas kernels, on_device(): pl.pallas_call(kernel, out_shape=jax.ShapeDtypeStruct(clip.shape, BF16),...  87.7 us
    unnamed x1, local copies, waits for them, and re-layouts  2.06 us

profile of v1, /device:TPU:8, one launch (start us, length us, event | category | flops | bytes accessed | tf_op | source)
XLA Modules:
  0.0 89.8 jit_solution(18643300458178195)
XLA Ops:
  0.0 87.7 %shard_map.37 = bf16[16,32,768]{2,1,0:T(8,128)(2,1)} custom-call(bf16[16,32,768]{2,1,0:T(8,128)(2,1)} %clip.1, bf16[4,768,768]{2,1,0:T(8,128)(2,1)} %w_space.1, bf16[4,768,768]{2,1,0:T(8,128)(2,1)} %w_time.1), custom_call_target="tpu_custom_call" | custom-call | tf_op jit(solution)/shard_map/pallas_call | solution.py:284
  87.7 2.1 %copy.5 = bf16[16,32,768]{2,1,0:T(8,128)(2,1)} copy(bf16[16,32,768]{2,1,0:T(8,128)(2,1)} %shard_map.37) | data formatting | bytes 1572864

commit v2 on v1

v2 whole, which is shorter than its diff:
```python
import functools
import math

import jax
import jax.numpy as jnp
from jax import lax
from jax.experimental import pallas as pl
from jax.experimental.pallas import tpu as pltpu
from jax.sharding import PartitionSpec as P

MESH = pl.DeviceIdType.MESH
HEAD = 64
LANES = 128
WIDTH = 768
PAIRS = WIDTH // LANES
SCALE = math.log2(math.e) / math.sqrt(HEAD)
BF16 = jnp.bfloat16
F32 = jnp.float32

Z_OFFS = [(dz, dc) for dz in (3, -3, 1, -1, 0, 2, -2, 4) for dc in (0, 1)]
OWN = 8
OTHERS = [slot for slot in range(16) if slot != OWN]
Z_INV = [Z_OFFS.index((dz if dz == 4 else -dz, dc)) for dz, dc in Z_OFFS]
T_OFFS = [(dx, dy) for dx in (0, 1, 3, 2) for dy in (0, 1, 3, 2)]
T_INV = [T_OFFS.index(((-dx) % 4, (-dy) % 4)) for dx, dy in T_OFFS]

A_SENDS = (9, 14, 15, 0, 2, 1, 3, 10, 12, 11, 13, 4, 6, 5, 7)
B_SENDS = ((0, 2, 1, 3, 4, 6, 5, 7), (14, 15, 10, 12, 11, 13, 9, 8))
Z_GROUPS = ((8, 10), (14, 16), (0, 4), (10, 14), (4, 8))


def z_peer(me, slot):
    dz, dc = Z_OFFS[slot]
    return lax.rem(me // 2 + (dz + 8), 8) * 2 + lax.rem(lax.rem(me, 2) + dc, 2)


def t_peer(me, slot):
    dx, dy = T_OFFS[slot]
    return lax.rem(me // 4 + dx, 4) * 4 + lax.rem(lax.rem(me, 4) + dy, 4)


def normed_rows(rows):
    wide = rows.astype(F32)
    return (wide * lax.rsqrt(jnp.mean(wide * wide, axis=-1, keepdims=True) + 1e-06)).astype(BF16)


def dot(a, b):
    return jnp.dot(a, b, preferred_element_type=F32)


def attend(q, k, vx, bias):
    n = q.shape[0] // 2
    scores = lax.dot_general(q, k, (((1,), (1,)), ((), ())), preferred_element_type=F32)
    if bias is not None:
        scores = scores + bias
    largest = jnp.max(scores, axis=-1, keepdims=True)
    expo = jnp.exp2(scores - largest).astype(BF16)
    both = dot(expo, vx)
    both = both[:, :LANES] / both[:, LANES:]
    lane = lax.broadcasted_iota(jnp.int32, (n, LANES), 1)
    return jnp.where(lane < HEAD, both[:n], both[n:]).astype(BF16)


def kernel(
    clip, w_space, w_time, out,
    ws, wt, x, q2, k, vx, mix, after, home, perm, unperm, bias0, bias1, grouped, series,
    tq2, tk, tvx, tmix, answer, back, final,
    w_sem, a_send, a_recv, b_send, b_recv, c_send, c_recv, d_send, d_recv, own_sem, out_sem,
):
    t_me = lax.axis_index("tm")
    s_me = lax.axis_index("space")

    loads = [pltpu.make_async_copy(w_space, ws, w_sem.at[0]), pltpu.make_async_copy(w_time, wt, w_sem.at[1])]
    own_a = pltpu.make_async_copy(clip.at[s_me], x.at[OWN], own_sem.at[0])
    own_a.start()
    for load in loads:
        load.start()

    barrier = pltpu.get_barrier_semaphore()
    for slot in reversed(A_SENDS):
        pl.semaphore_signal(barrier, inc=1, device_id={"space": z_peer(s_me, slot)}, device_id_type=MESH)
    for slot in range(15, 0, -1):
        pl.semaphore_signal(barrier, inc=1, device_id={"tm": t_peer(t_me, slot)}, device_id_type=MESH)
    pl.semaphore_wait(barrier, 30)

    def a_copy(slot):
        peer = z_peer(s_me, slot)
        return pltpu.make_async_remote_copy(
            src_ref=clip.at[peer], dst_ref=x.at[Z_INV[slot]],
            send_sem=a_send.at[slot], recv_sem=a_recv.at[Z_INV[slot]],
            device_id={"space": peer}, device_id_type=MESH,
        )

    for slot in A_SENDS:
        a_copy(slot).start()

    ones = jnp.ones((512, LANES), BF16)
    for pair in range(PAIRS):
        vx[pair, :, LANES:] = ones
        tvx[pair, :, :, LANES:] = ones[:256].reshape(2, 128, LANES)
    frames = [z_peer(s_me, slot) for slot in range(16)]

    def frame_of(slots):
        found = jnp.zeros_like(slots)
        for slot in range(16):
            found = jnp.where(slots == slot, frames[slot], found)
        return found

    row = lax.broadcasted_iota(jnp.int32, (128, 128), 0)
    col = lax.broadcasted_iota(jnp.int32, (128, 128), 1)
    perm[...] = jnp.where((row // 8 == col % 16) & (row % 8 == col // 16), 1.0, 0.0).astype(BF16)
    row = lax.broadcasted_iota(jnp.int32, (256, 256), 0)
    col = lax.broadcasted_iota(jnp.int32, (1, 256), 1)
    unperm[...] = jnp.where((row // 16 == frame_of(col % 16)) & (row % 16 == col // 16), 1.0, 0.0).astype(BF16)
    for half, bias in enumerate((bias0, bias1)):
        blocks = 8 * (half + 1)
        key = lax.broadcasted_iota(jnp.int32, (1, 16 * blocks), 1)
        key_at = key % (8 * blocks) // 8 * 16 + frame_of(key // (8 * blocks) * 8 + key % 8)
        query = lax.broadcasted_iota(jnp.int32, (256, 1), 0) % 128
        query_at = (query % 64 // 8 + 8 * half) * 16 + frame_of(query // 64 * 8 + query % 8)
        bias[...] = jnp.where(key_at <= query_at, 0.0, -1e30).astype(F32)
    lane = lax.broadcasted_iota(jnp.int32, (1, WIDTH), 1)
    first = jnp.where(lane % LANES < HEAD, SCALE, 0.0).astype(F32)
    second = jnp.where(lane % LANES < HEAD, 0.0, SCALE).astype(F32)

    loads[0].wait()
    own_a.wait()
    for lo, hi in Z_GROUPS:
        for slot in range(lo, hi):
            if slot == OWN:
                continue
            pltpu.make_async_remote_copy(
                src_ref=clip.at[0], dst_ref=x.at[slot], send_sem=a_send.at[slot], recv_sem=a_recv.at[slot],
                device_id={"space": z_peer(s_me, slot)}, device_id_type=MESH,
            ).wait_recv()
        count = hi - lo
        normed = normed_rows(x[lo:hi].reshape(count * 32, WIDTH))
        for index in range(3):
            made = dot(normed, ws[index])
            if index == 0:
                kinds = [((made * first).astype(BF16), q2, 0), ((made * second).astype(BF16), q2, 1)]
            else:
                kinds = [(made.astype(BF16), (k, vx)[index - 1], None)]
            for value, ref, head in kinds:
                value = value.reshape(count, 2, 16, WIDTH)
                for th in range(2):
                    part = value[:, th].reshape(count * 16, WIDTH)
                    at = pl.ds(th * 256 + lo * 16, count * 16)
                    for pair in range(PAIRS):
                        piece = part[:, pair * LANES:(pair + 1) * LANES]
                        if head is None:
                            ref[pair, at, :LANES] = piece
                        else:
                            ref[pair, head, at, :] = piece

    def b_copy(th, slot):
        peer = z_peer(s_me, slot)
        return pltpu.make_async_remote_copy(
            src_ref=after.at[th, slot], dst_ref=home.at[th, Z_INV[slot]],
            send_sem=b_send.at[th, slot], recv_sem=b_recv.at[th, Z_INV[slot]],
            device_id={"space": peer}, device_id_type=MESH,
        )

    def c_copy(th, part, slot):
        peer = t_peer(t_me, slot)
        return pltpu.make_async_remote_copy(
            src_ref=grouped.at[th, part, peer], dst_ref=series.at[th, part, t_me],
            send_sem=c_send.at[th, part, slot], recv_sem=c_recv.at[th, part, T_INV[slot]],
            device_id={"tm": peer}, device_id_type=MESH,
        )

    def d_copy(th, slot):
        peer = t_peer(t_me, slot)
        return pltpu.make_async_remote_copy(
            src_ref=answer.at[th, peer], dst_ref=back.at[th, t_me],
            send_sem=d_send.at[th, slot], recv_sem=d_recv.at[th, T_INV[slot]],
            device_id={"tm": peer}, device_id_type=MESH,
        )

    own_b = [pltpu.make_async_copy(after.at[th, OWN], home.at[th, OWN], own_sem.at[1 + th]) for th in range(2)]
    own_c = [
        [
            pltpu.make_async_copy(grouped.at[th, part, t_me], series.at[th, part, t_me], own_sem.at[3 + 2 * th + part])
            for part in range(2)
        ]
        for th in range(2)
    ]
    own_d = [pltpu.make_async_copy(answer.at[th, t_me], back.at[th, t_me], own_sem.at[7 + th]) for th in range(2)]

    def space_block(th, half):
        base = th * 256 + half * 128

        for pair in range(PAIRS):
            q = q2[pair, :, base:base + 128, :].reshape(256, LANES)
            mix[:, pair * LANES:(pair + 1) * LANES] = attend(q, k[pair], vx[pair], None)
        held = x[half * 8:half * 8 + 8, th * 16:th * 16 + 16, :].reshape(128, WIDTH).astype(F32)
        done = (held + dot(mix[...], ws[3])).astype(BF16)
        after[th, half * 8:half * 8 + 8] = done.reshape(8, 16, WIDTH)
        for slot in B_SENDS[half]:
            if slot == OWN:
                own_b[th].start()
            else:
                b_copy(th, slot).start()

    def regroup(th, part):
        for slot in range(8 * part, 8 * part + 8):
            if slot == OWN:
                own_b[th].wait()
            else:
                pltpu.make_async_remote_copy(
                    src_ref=after.at[th, slot], dst_ref=home.at[th, slot],
                    send_sem=b_send.at[th, slot], recv_sem=b_recv.at[th, slot],
                    device_id={"space": z_peer(s_me, slot)}, device_id_type=MESH,
                ).wait_recv()
        moved = dot(perm[...], home[th, 8 * part:8 * part + 8].reshape(128, WIDTH)).astype(BF16)
        grouped[th, part] = moved.reshape(16, 8, WIDTH)
        own_c[th][part].start()
        for slot in range(15, 0, -1):
            c_copy(th, part, slot).start()

    def time_project(th, part):
        own_c[th][part].wait()
        for slot in range(1, 16):
            pltpu.make_async_remote_copy(
                src_ref=grouped.at[th, part, 0], dst_ref=series.at[th, part, t_peer(t_me, slot)],
                send_sem=c_send.at[th, part, slot], recv_sem=c_recv.at[th, part, slot],
                device_id={"tm": t_peer(t_me, slot)}, device_id_type=MESH,
            ).wait_recv()
        normed = normed_rows(series[th, part].reshape(128, WIDTH))
        for index in range(3):
            made = dot(normed, wt[index])
            for pair in range(PAIRS):
                cols = slice(pair * LANES, (pair + 1) * LANES)
                if index == 0:
                    tq2[pair, 0, part] = (made[:, cols] * first[:, cols]).astype(BF16)
                    tq2[pair, 1, part] = (made[:, cols] * second[:, cols]).astype(BF16)
                elif index == 1:
                    tk[pair, part] = made[:, cols].astype(BF16)
                else:
                    tvx[pair, part, :, :LANES] = made[:, cols].astype(BF16)

    def time_block(th, half):
        rows = 64 * (half + 1)
        bias = (bias0, bias1)[half]
        for pair in range(PAIRS):
            q = tq2[pair, :, :, half * 64:half * 64 + 64, :].reshape(256, LANES)
            keys = tk[pair, :, :rows, :].reshape(2 * rows, LANES)
            values = tvx[pair, :, :rows, :].reshape(2 * rows, 2 * LANES)
            tmix[:, pair * LANES:(pair + 1) * LANES] = attend(q, keys, values, bias[...])
        held = series[th, :, half * 8:half * 8 + 8].reshape(128, WIDTH).astype(F32)
        done = held + dot(tmix[...], wt[3])
        done = jnp.swapaxes(done.reshape(2, 8, 8, WIDTH), 0, 1).reshape(8, 16, WIDTH)
        answer[th, half * 8:half * 8 + 8] = done.astype(BF16)

    def send_answer(th):
        own_d[th].start()
        for slot in range(15, 0, -1):
            d_copy(th, slot).start()

    outs = [
        pltpu.make_async_copy(final.at[th], out.at[:, pl.ds(th * 16, 16), :], out_sem.at[th]) for th in range(2)
    ]

    def finish(th):
        own_d[th].wait()
        for slot in range(1, 16):
            pltpu.make_async_remote_copy(
                src_ref=answer.at[th, 0], dst_ref=back.at[th, t_peer(t_me, slot)],
                send_sem=d_send.at[th, slot], recv_sem=d_recv.at[th, slot],
                device_id={"tm": t_peer(t_me, slot)}, device_id_type=MESH,
            ).wait_recv()
        moved = dot(unperm[...], back[th].reshape(256, WIDTH)).astype(BF16)
        final[th] = moved.reshape(16, 16, WIDTH)
        outs[th].start()

    for th in range(2):
        space_block(th, 0)
        space_block(th, 1)
    regroup(0, 0)
    regroup(0, 1)
    loads[1].wait()
    time_project(0, 0)
    time_project(0, 1)
    regroup(1, 0)
    time_block(0, 0)
    time_block(0, 1)
    regroup(1, 1)
    send_answer(0)
    time_project(1, 0)
    time_project(1, 1)
    time_block(1, 0)
    time_block(1, 1)
    send_answer(1)
    finish(0)
    finish(1)

    for slot in OTHERS:
        a_copy(slot).wait_send()
        for th in range(2):
            b_copy(th, slot).wait_send()
    for slot in range(1, 16):
        for th in range(2):
            for part in range(2):
                c_copy(th, part, slot).wait_send()
            d_copy(th, slot).wait_send()
    for copy in outs:
        copy.wait()


def on_device(clip, w_spatial, w_temporal):
    dma = pltpu.SemaphoreType.DMA
    vmem = pltpu.VMEM
    return pl.pallas_call(
        kernel,
        out_shape=jax.ShapeDtypeStruct(clip.shape, BF16),
        in_specs=[pl.BlockSpec(memory_space=pltpu.HBM)] * 3,
        out_specs=pl.BlockSpec(memory_space=pl.ANY),
        scratch_shapes=[
            vmem((4, WIDTH, WIDTH), BF16),
            vmem((4, WIDTH, WIDTH), BF16),
            vmem((16, 32, WIDTH), BF16),
            vmem((PAIRS, 2, 512, LANES), BF16),
            vmem((PAIRS, 512, LANES), BF16),
            vmem((PAIRS, 512, 2 * LANES), BF16),
            vmem((128, WIDTH), BF16),
            vmem((2, 16, 16, WIDTH), BF16),
            vmem((2, 16, 16, WIDTH), BF16),
            vmem((128, 128), BF16),
            vmem((256, 256), BF16),
            vmem((256, 128), F32),
            vmem((256, 256), F32),
            vmem((2, 2, 16, 8, WIDTH), BF16),
            vmem((2, 2, 16, 8, WIDTH), BF16),
            vmem((PAIRS, 2, 2, 128, LANES), BF16),
            vmem((PAIRS, 2, 128, LANES), BF16),
            vmem((PAIRS, 2, 128, 2 * LANES), BF16),
            vmem((128, WIDTH), BF16),
            vmem((2, 16, 16, WIDTH), BF16),
            vmem((2, 16, 16, WIDTH), BF16),
            vmem((2, 16, 16, WIDTH), BF16),
            dma((2,)),
            dma((16,)), dma((16,)),
            dma((2, 16)), dma((2, 16)),
            dma((2, 2, 16)), dma((2, 2, 16)),
            dma((2, 16)), dma((2, 16)),
            dma((9,)),
            dma((2,)),
        ],
        compiler_params=pltpu.CompilerParams(
            collective_id=0, has_side_effects=True, vmem_limit_bytes=40 * 1024 * 1024
        ),
    )(*(pltpu.with_memory_space_constraint(v, pltpu.HBM) for v in (clip, w_spatial, w_temporal)))


def solution(mesh):
    placed = (P("tm", "space", None), P(), P())
    return jax.shard_map(
        on_device, mesh=mesh, in_specs=placed, out_specs=P("tm", "space", None), check_vma=False
    )
```

time: 89.9 us -> 71.2 us (0.79)
  the two profiles are of different devices: /device:TPU:8 before, /device:TPU:34 now
where the time goes in v2:
time: 71.2 us; the launch traced here: 71.1 us
  Pallas kernels  70.2 us (99%)
  local copies, waits for them, and re-layouts  0.88 us (1%)
    pallas_call x1, Pallas kernels, on_device(): pl.pallas_call(kernel, out_shape=jax.ShapeDtypeStruct(clip.shape, BF16),...  70.2 us

profile of v2, /device:TPU:34, one launch (start us, length us, event | category | flops | bytes accessed | tf_op | source)
XLA Modules:
  0.0 71.1 jit_solution(2228748307579325755)
XLA Ops:
  0.0 70.2 %shard_map.37 = bf16[16,32,768]{2,1,0:T(8,128)(2,1)S(1)} custom-call(bf16[16,32,768]{2,1,0:T(8,128)(2,1)} %clip.1, bf16[4,768,768]{2,1,0:T(8,128)(2,1)} %w_space.1, bf16[4,768,768]{2,1,0:T(8,128)(2,1)} %w_time.1), custom_call_target="tpu_custom_call" | custom-call | tf_op jit(solution)/shard_map/pallas_call | solution.py:313
  70.2 0.9 %copy.5 = bf16[16,32,768]{2,1,0:T(8,128)(2,1)} copy(bf16[16,32,768]{2,1,0:T(8,128)(2,1)S(1)} %shard_map.37) | data formatting | bytes 1572864

commit v3 on v2

--- a/solution.py
+++ b/solution.py
@@ -17,21 +17,17 @@
 BF16 = jnp.bfloat16
 F32 = jnp.float32
 
-Z_OFFS = [(dz, dc) for dz in (3, -3, 1, -1, 0, 2, -2, 4) for dc in (0, 1)]
-OWN = 8
-OTHERS = [slot for slot in range(16) if slot != OWN]
-Z_INV = [Z_OFFS.index((dz if dz == 4 else -dz, dc)) for dz, dc in Z_OFFS]
+Z_OFFS = (4, 3, -3, 2, -2, 1, -1, 0)
+Z_INV = (0, 2, 1, 4, 3, 6, 5, 7)
+HERE = 7
 T_OFFS = [(dx, dy) for dx in (0, 1, 3, 2) for dy in (0, 1, 3, 2)]
 T_INV = [T_OFFS.index(((-dx) % 4, (-dy) % 4)) for dx, dy in T_OFFS]
 
-A_SENDS = (9, 14, 15, 0, 2, 1, 3, 10, 12, 11, 13, 4, 6, 5, 7)
-B_SENDS = ((0, 2, 1, 3, 4, 6, 5, 7), (14, 15, 10, 12, 11, 13, 9, 8))
-Z_GROUPS = ((8, 10), (14, 16), (0, 4), (10, 14), (4, 8))
-
-
-def z_peer(me, slot):
-    dz, dc = Z_OFFS[slot]
-    return lax.rem(me // 2 + (dz + 8), 8) * 2 + lax.rem(lax.rem(me, 2) + dc, 2)
+Z_GROUPS = ((7, 8), (0, 1), (1, 3), (3, 5), (5, 7))
+
+
+def z_peer(me, near, core):
+    return lax.rem(me // 2 + (Z_OFFS[near] + 8), 8) * 2 + core
 
 
 def t_peer(me, slot):
@@ -69,36 +65,45 @@
 ):
     t_me = lax.axis_index("tm")
     s_me = lax.axis_index("space")
+    core = lax.rem(s_me, 2)
 
     loads = [pltpu.make_async_copy(w_space, ws, w_sem.at[0]), pltpu.make_async_copy(w_time, wt, w_sem.at[1])]
-    own_a = pltpu.make_async_copy(clip.at[s_me], x.at[OWN], own_sem.at[0])
+    own_a = pltpu.make_async_copy(clip.at[s_me], x.at[core, HERE], own_sem.at[0])
     own_a.start()
     for load in loads:
         load.start()
 
     barrier = pltpu.get_barrier_semaphore()
-    for slot in reversed(A_SENDS):
-        pl.semaphore_signal(barrier, inc=1, device_id={"space": z_peer(s_me, slot)}, device_id_type=MESH)
+    for near in range(8):
+        for dest in (core, 1 - core):
+            if near != HERE or dest is not core:
+                pl.semaphore_signal(barrier, inc=1, device_id={"space": z_peer(s_me, near, dest)}, device_id_type=MESH)
     for slot in range(15, 0, -1):
         pl.semaphore_signal(barrier, inc=1, device_id={"tm": t_peer(t_me, slot)}, device_id_type=MESH)
     pl.semaphore_wait(barrier, 30)
 
-    def a_copy(slot):
-        peer = z_peer(s_me, slot)
+    def a_copy(near, dest):
+        peer = z_peer(s_me, near, dest)
         return pltpu.make_async_remote_copy(
-            src_ref=clip.at[peer], dst_ref=x.at[Z_INV[slot]],
-            send_sem=a_send.at[slot], recv_sem=a_recv.at[Z_INV[slot]],
+            src_ref=clip.at[peer], dst_ref=x.at[core, Z_INV[near]],
+            send_sem=a_send.at[dest, near], recv_sem=a_recv.at[core, Z_INV[near]],
             device_id={"space": peer}, device_id_type=MESH,
         )
 
-    for slot in A_SENDS:
-        a_copy(slot).start()
+    for dest in range(2):
+        for near in range(8):
+            if near == HERE:
+                @pl.when(core != dest)
+                def _():
+                    a_copy(near, dest).start()
+            else:
+                a_copy(near, dest).start()
 
     ones = jnp.ones((512, LANES), BF16)
     for pair in range(PAIRS):
         vx[pair, :, LANES:] = ones
         tvx[pair, :, :, LANES:] = ones[:256].reshape(2, 128, LANES)
-    frames = [z_peer(s_me, slot) for slot in range(16)]
+    frames = [z_peer(s_me, slot % 8, slot // 8) for slot in range(16)]
 
     def frame_of(slots):
         found = jnp.zeros_like(slots)
@@ -125,16 +130,23 @@
 
     loads[0].wait()
     own_a.wait()
+
+    def a_wait(near, source):
+        pltpu.make_async_remote_copy(
+            src_ref=clip.at[0], dst_ref=x.at[source, near],
+            send_sem=a_send.at[source, near], recv_sem=a_recv.at[source, near],
+            device_id={"space": z_peer(s_me, near, source)}, device_id_type=MESH,
+        ).wait_recv()
+
     for lo, hi in Z_GROUPS:
-        for slot in range(lo, hi):
-            if slot == OWN:
-                continue
-            pltpu.make_async_remote_copy(
-                src_ref=clip.at[0], dst_ref=x.at[slot], send_sem=a_send.at[slot], recv_sem=a_recv.at[slot],
-                device_id={"space": z_peer(s_me, slot)}, device_id_type=MESH,
-            ).wait_recv()
+        for near in range(lo, hi):
+            if near == HERE:
+                a_wait(near, 1 - core)
+            else:
+                a_wait(near, 0)
+                a_wait(near, 1)
         count = hi - lo
-        normed = normed_rows(x[lo:hi].reshape(count * 32, WIDTH))
+        normed = normed_rows(x[:, lo:hi].reshape(count * 64, WIDTH))
         for index in range(3):
             made = dot(normed, ws[index])
             if index == 0:
@@ -142,10 +154,10 @@
             else:
                 kinds = [(made.astype(BF16), (k, vx)[index - 1], None)]
             for value, ref, head in kinds:
-                value = value.reshape(count, 2, 16, WIDTH)
-                for th in range(2):
-                    part = value[:, th].reshape(count * 16, WIDTH)
-                    at = pl.ds(th * 256 + lo * 16, count * 16)
+                value = value.reshape(2, count, 2, 16, WIDTH)
+                for th, source in ((0, 0), (0, 1), (1, 0), (1, 1)):
+                    part = value[source, :, th].reshape(count * 16, WIDTH)
+                    at = pl.ds(th * 256 + source * 128 + lo * 16, count * 16)
                     for pair in range(PAIRS):
                         piece = part[:, pair * LANES:(pair + 1) * LANES]
                         if head is None:
@@ -153,13 +165,19 @@
                         else:
                             ref[pair, head, at, :] = piece
 
-    def b_copy(th, slot):
-        peer = z_peer(s_me, slot)
+    def b_copy(th, near, dest):
         return pltpu.make_async_remote_copy(
-            src_ref=after.at[th, slot], dst_ref=home.at[th, Z_INV[slot]],
-            send_sem=b_send.at[th, slot], recv_sem=b_recv.at[th, Z_INV[slot]],
-            device_id={"space": peer}, device_id_type=MESH,
+            src_ref=after.at[th, dest, near], dst_ref=home.at[th, core, Z_INV[near]],
+            send_sem=b_send.at[th, dest, near], recv_sem=b_recv.at[th, core, Z_INV[near]],
+            device_id={"space": z_peer(s_me, near, dest)}, device_id_type=MESH,
         )
+
+    def b_wait(th, near, source):
+        pltpu.make_async_remote_copy(
+            src_ref=after.at[th, source, near], dst_ref=home.at[th, source, near],
+            send_sem=b_send.at[th, source, near], recv_sem=b_recv.at[th, source, near],
+            device_id={"space": z_peer(s_me, near, source)}, device_id_type=MESH,
+        ).wait_recv()
 
     def c_copy(th, part, slot):
         peer = t_peer(t_me, slot)
@@ -177,7 +195,10 @@
             device_id={"tm": peer}, device_id_type=MESH,
         )
 
-    own_b = [pltpu.make_async_copy(after.at[th, OWN], home.at[th, OWN], own_sem.at[1 + th]) for th in range(2)]
+    own_b = [
+        pltpu.make_async_copy(after.at[th, core, HERE], home.at[th, core, HERE], own_sem.at[1 + th])
+        for th in range(2)
+    ]
     own_c = [
         [
             pltpu.make_async_copy(grouped.at[th, part, t_me], series.at[th, part, t_me], own_sem.at[3 + 2 * th + part])
@@ -193,26 +214,34 @@
         for pair in range(PAIRS):
             q = q2[pair, :, base:base + 128, :].reshape(256, LANES)
             mix[:, pair * LANES:(pair + 1) * LANES] = attend(q, k[pair], vx[pair], None)
-        held = x[half * 8:half * 8 + 8, th * 16:th * 16 + 16, :].reshape(128, WIDTH).astype(F32)
+        held = x[half, :, th * 16:th * 16 + 16, :].reshape(128, WIDTH).astype(F32)
         done = (held + dot(mix[...], ws[3])).astype(BF16)
-        after[th, half * 8:half * 8 + 8] = done.reshape(8, 16, WIDTH)
-        for slot in B_SENDS[half]:
-            if slot == OWN:
-                own_b[th].start()
-            else:
-                b_copy(th, slot).start()
+        after[th, half] = done.reshape(8, 16, WIDTH)
+        for near in range(8):
+            if near == HERE:
+                @pl.when(core == half)
+                def _():
+                    own_b[th].start()
+
+                @pl.when(core != half)
+                def _():
+                    b_copy(th, near, half).start()
+            else:
+                b_copy(th, near, half).start()
 
     def regroup(th, part):
-        for slot in range(8 * part, 8 * part + 8):
-            if slot == OWN:
-                own_b[th].wait()
-            else:
-                pltpu.make_async_remote_copy(
-                    src_ref=after.at[th, slot], dst_ref=home.at[th, slot],
-                    send_sem=b_send.at[th, slot], recv_sem=b_recv.at[th, slot],
-                    device_id={"space": z_peer(s_me, slot)}, device_id_type=MESH,
-                ).wait_recv()
-        moved = dot(perm[...], home[th, 8 * part:8 * part + 8].reshape(128, WIDTH)).astype(BF16)
+        for near in range(8):
+            if near == HERE:
+                @pl.when(core == part)
+                def _():
+                    own_b[th].wait()
+
+                @pl.when(core != part)
+                def _():
+                    b_wait(th, near, part)
+            else:
+                b_wait(th, near, part)
+        moved = dot(perm[...], home[th, part].reshape(128, WIDTH)).astype(BF16)
         grouped[th, part] = moved.reshape(16, 8, WIDTH)
         own_c[th][part].start()
         for slot in range(15, 0, -1):
@@ -276,15 +305,15 @@
     for th in range(2):
         space_block(th, 0)
         space_block(th, 1)
+    loads[1].wait()
     regroup(0, 0)
+    time_project(0, 0)
     regroup(0, 1)
-    loads[1].wait()
-    time_project(0, 0)
+    regroup(1, 0)
     time_project(0, 1)
-    regroup(1, 0)
+    regroup(1, 1)
     time_block(0, 0)
     time_block(0, 1)
-    regroup(1, 1)
     send_answer(0)
     time_project(1, 0)
     time_project(1, 1)
@@ -294,10 +323,12 @@
     finish(0)
     finish(1)
 
-    for slot in OTHERS:
-        a_copy(slot).wait_send()
-        for th in range(2):
-            b_copy(th, slot).wait_send()
+    for near in range(8):
+        for dest in (core, 1 - core):
+            if near != HERE or dest is not core:
+                a_copy(near, dest).wait_send()
+                b_copy(0, near, dest).wait_send()
+                b_copy(1, near, dest).wait_send()
     for slot in range(1, 16):
         for th in range(2):
             for part in range(2):
@@ -318,13 +349,13 @@
         scratch_shapes=[
             vmem((4, WIDTH, WIDTH), BF16),
             vmem((4, WIDTH, WIDTH), BF16),
-            vmem((16, 32, WIDTH), BF16),
+            vmem((2, 8, 32, WIDTH), BF16),
             vmem((PAIRS, 2, 512, LANES), BF16),
             vmem((PAIRS, 512, LANES), BF16),
             vmem((PAIRS, 512, 2 * LANES), BF16),
             vmem((128, WIDTH), BF16),
-            vmem((2, 16, 16, WIDTH), BF16),
-            vmem((2, 16, 16, WIDTH), BF16),
+            vmem((2, 2, 8, 16, WIDTH), BF16),
+            vmem((2, 2, 8, 16, WIDTH), BF16),
             vmem((128, 128), BF16),
             vmem((256, 256), BF16),
             vmem((256, 128), F32),
@@ -339,8 +370,8 @@
             vmem((2, 16, 16, WIDTH), BF16),
             vmem((2, 16, 16, WIDTH), BF16),
             dma((2,)),
-            dma((16,)), dma((16,)),
-            dma((2, 16)), dma((2, 16)),
+            dma((2, 8)), dma((2, 8)),
+            dma((2, 2, 8)), dma((2, 2, 8)),
             dma((2, 2, 16)), dma((2, 2, 16)),
             dma((2, 16)), dma((2, 16)),
             dma((9,)),

time: 71.2 us -> 66.7 us (0.937)
  the two profiles are of different devices: /device:TPU:34 before, /device:TPU:1 now
where the time goes in v3:
time: 66.7 us; the launch traced here: 66.6 us
  Pallas kernels  65.7 us (99%)
  local copies, waits for them, and re-layouts  0.88 us (1%)
    pallas_call x1, Pallas kernels, on_device(): pl.pallas_call(kernel, out_shape=jax.ShapeDtypeStruct(clip.shape, BF16),...  65.7 us

profile of v3, /device:TPU:1, one launch (start us, length us, event | category | flops | bytes accessed | tf_op | source)
XLA Modules:
  0.0 66.6 jit_solution(10848384760194985558)
XLA Ops:
  0.0 65.7 %shard_map.37 = bf16[16,32,768]{2,1,0:T(8,128)(2,1)S(1)} custom-call(bf16[16,32,768]{2,1,0:T(8,128)(2,1)} %clip.1, bf16[4,768,768]{2,1,0:T(8,128)(2,1)} %w_space.1, bf16[4,768,768]{2,1,0:T(8,128)(2,1)} %w_time.1), custom_call_target="tpu_custom_call" | custom-call | tf_op jit(solution)/shard_map/pallas_call | solution.py:344
  65.7 0.9 %copy.5 = bf16[16,32,768]{2,1,0:T(8,128)(2,1)} copy(bf16[16,32,768]{2,1,0:T(8,128)(2,1)S(1)} %shard_map.37) | data formatting | bytes 1572864

commit v4 on v3

--- a/solution.py
+++ b/solution.py
@@ -21,6 +21,8 @@
 Z_INV = (0, 2, 1, 4, 3, 6, 5, 7)
 HERE = 7
 T_OFFS = [(dx, dy) for dx in (0, 1, 3, 2) for dy in (0, 1, 3, 2)]
+Y_STEPS = tuple(T_OFFS.index((0, dy)) for dy in (1, 3, 2))
+X_STEPS = tuple(T_OFFS.index((dx, 0)) for dx in (1, 3, 2))
 T_INV = [T_OFFS.index(((-dx) % 4, (-dy) % 4)) for dx, dy in T_OFFS]
 
 Z_GROUPS = ((7, 8), (0, 1), (1, 3), (3, 5), (5, 7))
@@ -60,8 +62,8 @@
 def kernel(
     clip, w_space, w_time, out,
     ws, wt, x, q2, k, vx, mix, after, home, perm, unperm, bias0, bias1, grouped, series,
-    tq2, tk, tvx, tmix, answer, back, final,
-    w_sem, a_send, a_recv, b_send, b_recv, c_send, c_recv, d_send, d_recv, own_sem, out_sem,
+    tq2, tk, tvx, tmix, answer, back,
+    w_sem, a_send, a_recv, b_send, b_recv, c_send, c_recv, d_send, d_recv, own_sem, y_sem, x_sem, all_sem,
 ):
     t_me = lax.axis_index("tm")
     s_me = lax.axis_index("space")
@@ -78,9 +80,13 @@
         for dest in (core, 1 - core):
             if near != HERE or dest is not core:
                 pl.semaphore_signal(barrier, inc=1, device_id={"space": z_peer(s_me, near, dest)}, device_id_type=MESH)
-    for slot in range(15, 0, -1):
+    for slot in (Y_STEPS[0], Y_STEPS[1], X_STEPS[0], X_STEPS[1]):
         pl.semaphore_signal(barrier, inc=1, device_id={"tm": t_peer(t_me, slot)}, device_id_type=MESH)
-    pl.semaphore_wait(barrier, 30)
+    pl.semaphore_wait(barrier, 19)
+    for slot in Y_STEPS[:2]:
+        pl.semaphore_signal(y_sem, inc=1, device_id={"tm": t_peer(t_me, slot)}, device_id_type=MESH)
+    for slot in X_STEPS[:2]:
+        pl.semaphore_signal(x_sem, inc=1, device_id={"tm": t_peer(t_me, slot)}, device_id_type=MESH)
 
     def a_copy(near, dest):
         peer = z_peer(s_me, near, dest)
@@ -286,10 +292,6 @@
         for slot in range(15, 0, -1):
             d_copy(th, slot).start()
 
-    outs = [
-        pltpu.make_async_copy(final.at[th], out.at[:, pl.ds(th * 16, 16), :], out_sem.at[th]) for th in range(2)
-    ]
-
     def finish(th):
         own_d[th].wait()
         for slot in range(1, 16):
@@ -299,13 +301,17 @@
                 device_id={"tm": t_peer(t_me, slot)}, device_id_type=MESH,
             ).wait_recv()
         moved = dot(unperm[...], back[th].reshape(256, WIDTH)).astype(BF16)
-        final[th] = moved.reshape(16, 16, WIDTH)
-        outs[th].start()
-
+        out[:, th * 16:th * 16 + 16, :] = moved.reshape(16, 16, WIDTH)
+
+    pl.semaphore_wait(y_sem, 2)
+    pl.semaphore_wait(x_sem, 2)
+    for slot in Y_STEPS:
+        pl.semaphore_signal(all_sem, inc=1, device_id={"tm": t_peer(t_me, slot)}, device_id_type=MESH)
     for th in range(2):
         space_block(th, 0)
         space_block(th, 1)
     loads[1].wait()
+    pl.semaphore_wait(all_sem, 3)
     regroup(0, 0)
     time_project(0, 0)
     regroup(0, 1)
@@ -334,8 +340,6 @@
             for part in range(2):
                 c_copy(th, part, slot).wait_send()
             d_copy(th, slot).wait_send()
-    for copy in outs:
-        copy.wait()
 
 
 def on_device(clip, w_spatial, w_temporal):
@@ -345,7 +349,7 @@
         kernel,
         out_shape=jax.ShapeDtypeStruct(clip.shape, BF16),
         in_specs=[pl.BlockSpec(memory_space=pltpu.HBM)] * 3,
-        out_specs=pl.BlockSpec(memory_space=pl.ANY),
+        out_specs=pl.BlockSpec(memory_space=pltpu.VMEM),
         scratch_shapes=[
             vmem((4, WIDTH, WIDTH), BF16),
             vmem((4, WIDTH, WIDTH), BF16),
@@ -368,14 +372,15 @@
             vmem((128, WIDTH), BF16),
             vmem((2, 16, 16, WIDTH), BF16),
             vmem((2, 16, 16, WIDTH), BF16),
-            vmem((2, 16, 16, WIDTH), BF16),
             dma((2,)),
             dma((2, 8)), dma((2, 8)),
             dma((2, 2, 8)), dma((2, 2, 8)),
             dma((2, 2, 16)), dma((2, 2, 16)),
             dma((2, 16)), dma((2, 16)),
             dma((9,)),
-            dma((2,)),
+            pltpu.SemaphoreType.REGULAR,
+            pltpu.SemaphoreType.REGULAR,
+            pltpu.SemaphoreType.REGULAR,
         ],
         compiler_params=pltpu.CompilerParams(
             collective_id=0, has_side_effects=True, vmem_limit_bytes=40 * 1024 * 1024

time: 66.7 us -> 66.2 us (level)
  no operation moved by 1% of the time
where the time goes in v4:
time: 66.2 us; the launch traced here: 66.1 us
  Pallas kernels  65.2 us (98%)
  local copies, waits for them, and re-layouts  0.88 us (1%)
    pallas_call x1, Pallas kernels, on_device(): pl.pallas_call(kernel, out_shape=jax.ShapeDtypeStruct(clip.shape, BF16),...  65.2 us

profile of v4, /device:TPU:1, one launch (start us, length us, event | category | flops | bytes accessed | tf_op | source)
XLA Modules:
  0.0 66.1 jit_solution(15833683409033100719)
XLA Ops:
  0.0 65.2 %shard_map.37 = bf16[16,32,768]{2,1,0:T(8,128)(2,1)S(1)} custom-call(bf16[16,32,768]{2,1,0:T(8,128)(2,1)} %clip.1, bf16[4,768,768]{2,1,0:T(8,128)(2,1)} %w_space.1, bf16[4,768,768]{2,1,0:T(8,128)(2,1)} %w_time.1), custom_call_target="tpu_custom_call" | custom-call | tf_op jit(solution)/shard_map/pallas_call | solution.py:348
  65.2 0.9 %copy.5 = bf16[16,32,768]{2,1,0:T(8,128)(2,1)} copy(bf16[16,32,768]{2,1,0:T(8,128)(2,1)S(1)} %shard_map.37) | data formatting | bytes 1572864

commit v5 on v4

--- a/solution.py
+++ b/solution.py
@@ -281,13 +281,15 @@
             q = tq2[pair, :, :, half * 64:half * 64 + 64, :].reshape(256, LANES)
             keys = tk[pair, :, :rows, :].reshape(2 * rows, LANES)
             values = tvx[pair, :, :rows, :].reshape(2 * rows, 2 * LANES)
-            tmix[:, pair * LANES:(pair + 1) * LANES] = attend(q, keys, values, bias[...])
-        held = series[th, :, half * 8:half * 8 + 8].reshape(128, WIDTH).astype(F32)
-        done = held + dot(tmix[...], wt[3])
-        done = jnp.swapaxes(done.reshape(2, 8, 8, WIDTH), 0, 1).reshape(8, 16, WIDTH)
-        answer[th, half * 8:half * 8 + 8] = done.astype(BF16)
+            tmix[half * 128:half * 128 + 128, pair * LANES:(pair + 1) * LANES] = attend(q, keys, values, bias[...])
 
     def send_answer(th):
+        made = dot(tmix[...], wt[3])
+        for half in range(2):
+            held = series[th, :, half * 8:half * 8 + 8].reshape(128, WIDTH).astype(F32)
+            done = held + made[half * 128:half * 128 + 128]
+            done = jnp.swapaxes(done.reshape(2, 8, 8, WIDTH), 0, 1).reshape(8, 16, WIDTH)
+            answer[th, half * 8:half * 8 + 8] = done.astype(BF16)
         own_d[th].start()
         for slot in range(15, 0, -1):
             d_copy(th, slot).start()
@@ -369,7 +371,7 @@
             vmem((PAIRS, 2, 2, 128, LANES), BF16),
             vmem((PAIRS, 2, 128, LANES), BF16),
             vmem((PAIRS, 2, 128, 2 * LANES), BF16),
-            vmem((128, WIDTH), BF16),
+            vmem((256, WIDTH), BF16),
             vmem((2, 16, 16, WIDTH), BF16),
             vmem((2, 16, 16, WIDTH), BF16),
             dma((2,)),

time: 66.2 us -> 65.9 us (level)
  no operation moved by 1% of the time
where the time goes in v5:
time: 65.9 us; the launch traced here: 65.8 us
  Pallas kernels  64.9 us (98%)
  local copies, waits for them, and re-layouts  0.88 us (1%)
    pallas_call x1, Pallas kernels, on_device(): pl.pallas_call(kernel, out_shape=jax.ShapeDtypeStruct(clip.shape, BF16),...  64.9 us

profile of v5, /device:TPU:1, one launch (start us, length us, event | category | flops | bytes accessed | tf_op | source)
XLA Modules:
  0.0 65.8 jit_solution(7399442825253715266)
XLA Ops:
  0.0 64.9 %shard_map.37 = bf16[16,32,768]{2,1,0:T(8,128)(2,1)S(1)} custom-call(bf16[16,32,768]{2,1,0:T(8,128)(2,1)} %clip.1, bf16[4,768,768]{2,1,0:T(8,128)(2,1)} %w_space.1, bf16[4,768,768]{2,1,0:T(8,128)(2,1)} %w_time.1), custom_call_target="tpu_custom_call" | custom-call | tf_op jit(solution)/shard_map/pallas_call | solution.py:350
  65.0 0.9 %copy.5 = bf16[16,32,768]{2,1,0:T(8,128)(2,1)} copy(bf16[16,32,768]{2,1,0:T(8,128)(2,1)S(1)} %shard_map.37) | data formatting | bytes 1572864
